TPU v7x, 32 devices: a whole 2x2x4 slice. The times are simulated.
32 devices in a mesh: dp: 16 (over z, x, core), tensor: 2 (over y).
Axes of the slice: x: 2, y: 2, z: 4, core: 2. Of those that a mesh axis runs over, the one named last changes fastest.
Arguments:
- tokens: bfloat16 [37632, 768], P(('dp', 'tensor')), may hold values from -6 to 6
- cotangent: bfloat16 [37632, 768], P(('dp', 'tensor')), may hold values from -6 to 6
- window_extent: int32 [768, 2], P('dp'), may hold values from 1 to 7, as said below
- norm1_gain: float32 [768], replicated, may hold values from 0.25 to 1.75
- norm1_shift: float32 [768], replicated, may hold values from -1.25 to 1.25
- qkv_weight: bfloat16 [768, 3, 768], P(None, None, 'tensor'), may hold values from -0.21875 to 0.21875
- query_value_bias: float32 [2, 768], P(None, 'tensor'), may hold values from -1.75 to 1.75
- relative_bias: float32 [169, 24], P(None, 'tensor'), may hold values from -6 to 6
- proj_weight: bfloat16 [768, 768], P('tensor'), may hold values from -0.875 to 0.875
- proj_bias: float32 [768], replicated, may hold values from -1.75 to 1.75
- norm2_gain: float32 [768], replicated, may hold values from 0.25 to 1.75
- norm2_shift: float32 [768], replicated, may hold values from -1.25 to 1.25
- up_weight: bfloat16 [768, 3072], P(None, 'tensor'), may hold values from -0.21875 to 0.21875
- up_bias: float32 [3072], P('tensor'), may hold values from -1.75 to 1.75
- down_weight: bfloat16 [3072, 768], P('tensor'), may hold values from -0.15625 to 0.15625
- down_bias: float32 [768], replicated, may hold values from -1.75 to 1.75
Outputs:
- block_out: bfloat16 [37632, 768], P(('dp', 'tensor'))
- tokens_grad: float32 [37632, 768], P(('dp', 'tensor'))
- norm1_gain_grad: float32 [768], replicated
- norm1_shift_grad: float32 [768], replicated
- qkv_weight_grad: float32 [768, 3, 768], P(None, None, 'tensor')
- query_value_bias_grad: float32 [2, 768], P(None, 'tensor')
- relative_bias_grad: float32 [169, 24], P(None, 'tensor')
- proj_weight_grad: float32 [768, 768], P('tensor')
- proj_bias_grad: float32 [768], replicated
- norm2_gain_grad: float32 [768], replicated
- norm2_shift_grad: float32 [768], replicated
- up_weight_grad: float32 [768, 3072], P(None, 'tensor')
- up_bias_grad: float32 [3072], P('tensor')
- down_weight_grad: float32 [3072, 768], P('tensor')
- down_bias_grad: float32 [768], replicated
Inputs may be any that keep to these rules, and one draw needn't show every extreme that they name: `window_extent`: windows come in aligned groups of four. A group holds either four images of 7 x 7 patches, each extent (7, 7), or the four windows of one image of 8 x 7 + 1 patches padded to 14 x 2 * 7, with extents (7, 7), (7, 1), (1, 7), (1, 1) in that order.
All inputs are finite; a program needn't handle non-finite values.
Results may differ from a plain program's by a relative error of at most 0.017.
Values may be sent and summed in bfloat16 or wider, within the bound.
No kernel may reach another device: no remote copies, remote signals or barrier semaphores. Data moves between devices by JAX's collectives and lax.ppermute only.
A program may use at most 192 MiB of HBM per device.

v0:
```python
import math

import jax
import jax.numpy as jnp
from jax import lax
from jax.sharding import PartitionSpec as P

WIN = 7


norm_epsilon = 1e-05
masked_score = -1e30
highest = lax.Precision.HIGHEST


def window_masks(window_extent):
    places = jnp.arange(WIN * WIN, dtype=jnp.int32)
    rows_at = places // WIN
    cols_at = places % WIN
    return (rows_at[None, :] < window_extent[:, 0:1]) & (cols_at[None, :] < window_extent[:, 1:2])


def relative_onehot():
    places = jnp.arange(WIN * WIN, dtype=jnp.int32)
    rows_at = places // WIN
    cols_at = places % WIN
    index = (
        (rows_at[:, None] - rows_at[None, :] + WIN - 1) * (2 * WIN - 1)
        + cols_at[:, None]
        - cols_at[None, :]
        + WIN
        - 1
    )
    slots = jnp.arange((2 * WIN - 1) ** 2, dtype=jnp.int32)
    return (index.reshape(-1)[:, None] == slots[None, :]).astype(jnp.float32)


def head_bias(onehot, table):
    heads = table.shape[1]
    flat = jnp.dot(onehot, table, precision=highest, preferred_element_type=jnp.float32)
    return flat.T.reshape(heads, WIN * WIN, WIN * WIN)


def norm_forward(values, gain, shift):
    center = values - jnp.mean(values, axis=-1, keepdims=True)
    inverse = lax.rsqrt(jnp.mean(center * center, axis=-1, keepdims=True) + norm_epsilon)
    unit = center * inverse
    return (unit * gain + shift, unit, inverse)


def norm_backward(normed_grad, unit, inverse, gain):
    unit_grad = normed_grad * gain
    inputs_grad = inverse * (
        unit_grad
        - jnp.mean(unit_grad, axis=-1, keepdims=True)
        - unit * jnp.mean(unit_grad * unit, axis=-1, keepdims=True)
    )
    return (inputs_grad, jnp.sum(normed_grad * unit, axis=0), jnp.sum(normed_grad, axis=0))


def gelu_parts(hidden):
    cdf = 0.5 * (1.0 + lax.erf(hidden * 0.7071067811865476))
    slope = cdf + hidden * jnp.exp(-0.5 * hidden * hidden) * 0.3989422804014327
    return (hidden * cdf, slope)


def product(left, right, left_dim, right_dim):
    return lax.dot_general(
        left, right, (((left_dim,), (right_dim,)), ((), ())), preferred_element_type=jnp.float32
    )


def slice_product(left, right, contract):
    return product(left, right, 1, contract)


def block_layout(queries, key_mask, heads):
    windows = key_mask.shape[0]
    per_block = math.gcd(windows, 12)
    count = windows // per_block
    size = queries.shape[1] // heads
    return ((count, per_block, WIN * WIN, heads, size), (count, per_block, WIN * WIN), size)


def block_scores(query_blk, key_blk, mask_blk, bias_full, size):
    scores = jnp.einsum("wihd,wjhd->whij", query_blk, key_blk, preferred_element_type=jnp.float32)
    scores = scores * size ** (-0.5) + bias_full[None]
    return jnp.where(mask_blk[:, None, None, :], scores, masked_score)


def attention_forward(queries, key_rows, value_rows, key_mask, bias_full):
    shape, mask_shape, size = block_layout(queries, key_mask, bias_full.shape[0])

    def one_block(pieces):
        query_blk, key_blk, value_blk, mask_blk = pieces
        scores = block_scores(query_blk, key_blk, mask_blk, bias_full, size)
        top = jnp.max(scores, axis=-1, keepdims=True)
        weights = jnp.exp(scores - top)
        total = jnp.sum(weights, axis=-1, keepdims=True)
        probs = (weights / total).astype(jnp.bfloat16)
        attended = jnp.einsum(
            "whij,wjhd->wihd", probs, value_blk, preferred_element_type=jnp.float32
        )
        return (attended.astype(jnp.bfloat16), top[..., 0] + jnp.log(total[..., 0]))

    attended, logsum = lax.map(
        one_block,
        (
            queries.reshape(shape),
            key_rows.reshape(shape),
            value_rows.reshape(shape),
            key_mask.reshape(mask_shape),
        ),
    )
    return (attended.reshape(queries.shape), logsum)


def attention_backward(queries, key_rows, value_rows, key_mask, bias_full, logsum, attended_grad):
    heads = bias_full.shape[0]
    shape, mask_shape, size = block_layout(queries, key_mask, heads)
    scale = size ** (-0.5)

    def one_block(carry, pieces):
        query_blk, key_blk, value_blk, mask_blk, logsum_blk, grad_blk = pieces
        scores = block_scores(query_blk, key_blk, mask_blk, bias_full, size)
        probs = jnp.exp(scores - logsum_blk[..., None])
        probs_grad = jnp.einsum(
            "wihd,wjhd->whij", grad_blk, value_blk, preferred_element_type=jnp.float32
        )
        value_grad = jnp.einsum(
            "whij,wihd->wjhd",
            probs.astype(jnp.bfloat16),
            grad_blk,
            preferred_element_type=jnp.float32,
        )
        inner = jnp.sum(probs_grad * probs, axis=-1, keepdims=True)
        score_grad = (probs * (probs_grad - inner)).astype(jnp.bfloat16)
        query_grad = (
            jnp.einsum("whij,wjhd->wihd", score_grad, key_blk, preferred_element_type=jnp.float32)
            * scale
        )
        key_grad = (
            jnp.einsum("whij,wihd->wjhd", score_grad, query_blk, preferred_element_type=jnp.float32)
            * scale
        )
        return (
            carry + jnp.sum(score_grad.astype(jnp.float32), axis=0),
            (query_grad, key_grad, value_grad),
        )

    start = jnp.zeros((heads, WIN * WIN, WIN * WIN), jnp.float32)
    bias_grad, (query_grad, key_grad, value_grad) = lax.scan(
        one_block,
        start,
        (
            queries.reshape(shape),
            key_rows.reshape(shape),
            value_rows.reshape(shape),
            key_mask.reshape(mask_shape),
            logsum,
            attended_grad.reshape(shape),
        ),
    )
    return (
        query_grad.reshape(queries.shape),
        key_grad.reshape(queries.shape),
        value_grad.reshape(queries.shape),
        bias_grad,
    )


def local(
    tokens,
    cotangent,
    window_extent,
    norm1_gain,
    norm1_shift,
    qkv_weight,
    query_value_bias,
    relative_bias,
    proj_weight,
    proj_bias,
    norm2_gain,
    norm2_shift,
    up_weight,
    up_bias,
    down_weight,
    down_bias,
):
    width = tokens.shape[1]
    key_mask = window_masks(window_extent)
    own_windows = key_mask.shape[0] // lax.axis_size("tensor")
    own_mask = lax.dynamic_slice_in_dim(
        key_mask, lax.axis_index("tensor") * own_windows, own_windows, 0
    )
    row_mask = own_mask.reshape(-1, 1).astype(jnp.float32)
    onehot = relative_onehot()
    inputs = tokens.astype(jnp.float32)
    normed1, unit1, inverse1 = norm_forward(inputs, norm1_gain, norm1_shift)
    normed1_low = normed1.astype(jnp.bfloat16)
    attn_in = lax.all_gather(normed1_low, "tensor", axis=0, tiled=True)
    qkv_local, bias_local, table_local, proj_local = (
        qkv_weight,
        query_value_bias,
        relative_bias,
        proj_weight,
    )
    local_width = qkv_local.shape[2]
    qkv_flat = qkv_local.reshape(width, 3 * local_width)
    mixed = jnp.dot(attn_in, qkv_flat, preferred_element_type=jnp.float32).reshape(
        -1, 3, local_width
    )
    queries = (mixed[:, 0] + bias_local[0]).astype(jnp.bfloat16)
    key_rows = mixed[:, 1].astype(jnp.bfloat16)
    value_rows = (mixed[:, 2] + bias_local[1]).astype(jnp.bfloat16)
    bias_full = head_bias(onehot, table_local)
    attended, logsum = attention_forward(queries, key_rows, value_rows, key_mask, bias_full)
    branch = lax.psum_scatter(
        slice_product(attended, proj_local, 0).astype(jnp.bfloat16),
        "tensor",
        scatter_dimension=0,
        tiled=True,
    ).astype(jnp.float32)
    residual = inputs + branch + proj_bias
    normed2, unit2, inverse2 = norm_forward(residual, norm2_gain, norm2_shift)
    normed2_low = normed2.astype(jnp.bfloat16)
    mlp_in = lax.all_gather(normed2_low, "tensor", axis=0, tiled=True)
    up_local, up_bias_local, down_local = (up_weight, up_bias, down_weight)
    hidden = jnp.dot(mlp_in, up_local, preferred_element_type=jnp.float32) + up_bias_local
    activation, slope = gelu_parts(hidden)
    activation_low = activation.astype(jnp.bfloat16)
    down = lax.psum_scatter(
        slice_product(activation_low, down_local, 0).astype(jnp.bfloat16),
        "tensor",
        scatter_dimension=0,
        tiled=True,
    ).astype(jnp.float32)
    block_out = (row_mask * (residual + down + down_bias)).astype(jnp.bfloat16)
    out_grad = row_mask * cotangent.astype(jnp.float32)
    down_bias_grad = jnp.sum(out_grad, axis=0)
    out_low = out_grad.astype(jnp.bfloat16)
    down_in = lax.all_gather(out_low, "tensor", axis=0, tiled=True)
    activation_grad = product(down_in, down_local, 1, 1)
    down_weight_grad = product(activation_low, down_in, 0, 0)
    hidden_grad = activation_grad * slope
    up_bias_grad = jnp.sum(hidden_grad, axis=0)
    hidden_low = hidden_grad.astype(jnp.bfloat16)
    up_weight_grad = product(mlp_in, hidden_low, 0, 0)
    normed2_grad = lax.psum_scatter(
        slice_product(hidden_low, up_local, 1).astype(jnp.bfloat16),
        "tensor",
        scatter_dimension=0,
        tiled=True,
    ).astype(jnp.float32)
    residual_part, norm2_gain_grad, norm2_shift_grad = norm_backward(
        normed2_grad, unit2, inverse2, norm2_gain
    )
    residual_grad = out_grad + residual_part
    proj_bias_grad = jnp.sum(residual_grad, axis=0)
    residual_low = residual_grad.astype(jnp.bfloat16)
    branch_in = lax.all_gather(residual_low, "tensor", axis=0, tiled=True)
    attended_grad = product(branch_in, proj_local, 1, 1).astype(jnp.bfloat16)
    proj_weight_grad = product(attended, branch_in, 0, 0)
    query_grad, key_grad, value_grad, bias_grad = attention_backward(
        queries, key_rows, value_rows, key_mask, bias_full, logsum, attended_grad
    )
    query_value_bias_grad = jnp.stack([jnp.sum(query_grad, axis=0), jnp.sum(value_grad, axis=0)])
    mixed_grad = jnp.stack([query_grad, key_grad, value_grad], axis=1).astype(jnp.bfloat16)
    mixed_grad = mixed_grad.reshape(-1, 3 * local_width)
    qkv_weight_grad = product(attn_in, mixed_grad, 0, 0).reshape(width, 3, local_width)
    heads_here = bias_grad.shape[0]
    relative_bias_grad = lax.dot_general(
        onehot,
        bias_grad.reshape(heads_here, -1),
        (((0,), (1,)), ((), ())),
        precision=highest,
        preferred_element_type=jnp.float32,
    )
    normed1_grad = lax.psum_scatter(
        slice_product(mixed_grad, qkv_flat, 1).astype(jnp.bfloat16),
        "tensor",
        scatter_dimension=0,
        tiled=True,
    ).astype(jnp.float32)
    tokens_part, norm1_gain_grad, norm1_shift_grad = norm_backward(
        normed1_grad, unit1, inverse1, norm1_gain
    )
    tokens_grad = residual_grad + tokens_part
    (
        qkv_weight_grad,
        query_value_bias_grad,
        relative_bias_grad,
        proj_weight_grad,
        up_weight_grad,
        up_bias_grad,
        down_weight_grad,
    ) = lax.psum(
        (
            qkv_weight_grad,
            query_value_bias_grad,
            relative_bias_grad,
            proj_weight_grad,
            up_weight_grad,
            up_bias_grad,
            down_weight_grad,
        ),
        "dp",
    )
    (
        norm1_gain_grad,
        norm1_shift_grad,
        proj_bias_grad,
        norm2_gain_grad,
        norm2_shift_grad,
        down_bias_grad,
    ) = lax.psum(
        (
            norm1_gain_grad,
            norm1_shift_grad,
            proj_bias_grad,
            norm2_gain_grad,
            norm2_shift_grad,
            down_bias_grad,
        ),
        ("dp", "tensor"),
    )
    return (
        block_out,
        tokens_grad,
        norm1_gain_grad,
        norm1_shift_grad,
        qkv_weight_grad,
        query_value_bias_grad,
        relative_bias_grad,
        proj_weight_grad,
        proj_bias_grad,
        norm2_gain_grad,
        norm2_shift_grad,
        up_weight_grad,
        up_bias_grad,
        down_weight_grad,
        down_bias_grad,
    )


def solution(mesh):
    return jax.shard_map(
        local,
        mesh=mesh,
        in_specs=(
            P(("dp", "tensor"), None),
            P(("dp", "tensor"), None),
            P("dp", None),
            P(),
            P(),
            P(None, None, "tensor"),
            P(None, "tensor"),
            P(None, "tensor"),
            P("tensor", None),
            P(),
            P(),
            P(),
            P(None, "tensor"),
            P("tensor"),
            P("tensor", None),
            P(),
        ),
        out_specs=(
            P(("dp", "tensor"), None),
            P(("dp", "tensor"), None),
            P(),
            P(),
            P(None, None, "tensor"),
            P(None, "tensor"),
            P(None, "tensor"),
            P("tensor", None),
            P(),
            P(),
            P(),
            P(None, "tensor"),
            P("tensor"),
            P("tensor", None),
            P(),
        ),
        check_vma=False,
    )
```

profile of v0, /device:TPU:0, one launch (start us, length us, event | category | flops | bytes accessed | tf_op | source)
XLA Modules:
  0.0 1093.6 jit_solution(14763353908823860860)
XLA Ops:
  19.9 47.2 %all-gather.5.cloned.1.call-done = bf16[2352,768]{1,0:T(8,128)(2,1)} async-done(((bf16[1176,768]{1,0:T(8,128)(2,1)}), bf16[2352,768]{1,0:T(8,128)(2,1)}) %all-gather.5.cloned.1.call-update) | async-done | bytes 3612688 | tf_op jit(solution)/shard_map/all_gather | solution.py:201
  93.9 16.2 %convert_element_type.110 = bf16[4,12,49,12,32]{2,1,0,4,3:T(8,128)(2,1)} reshape(bf16[2352,1,384]{0,2,1:T(8,128)(2,1)} %copy.108) | data formatting | bytes 3612672 | tf_op jit(solution)/shard_map/convert_element_type | solution.py:214
  118.1 15.5 %squeeze.34 = f32[4,12,49,12,32]{2,1,0,4,3:T(8,128)} reshape(f32[2352,1,384]{0,2,1:T(8,128)} %copy.106) | data formatting | bytes 7225344 | tf_op jit(solution)/shard_map/squeeze | solution.py:215
  149.8 15.7 %squeeze.35 = f32[4,12,49,12,32]{2,1,0,4,3:T(8,128)} reshape(f32[2352,1,384]{0,2,1:T(8,128)} %copy.107) | data formatting | bytes 7225344 | tf_op jit(solution)/shard_map/squeeze | solution.py:213
  181.8 40.0 %while.29 = (s32[]{:T(128)}, bf16[4,12,49,12,32]{2,4,3,1,0:T(8,128)(2,1)}, f32[4,12,12,49]{3,2,1,0:T(8,128)}, bf16[4,12,49,12,32]{2,4,3,1,0:T(8,128)(2,1)}, pred...) while((s32[]{:T(128)}, ...), condition=%wide.region_5.6_spmd, body=%wide.region_2.5_spmd.sunk | while | flops 49660128 | bytes 9975225 | solution.py:106
  244.7 48.6 %reduce-scatter.5.cloned.1.call-done = bf16[1176,768]{1,0:T(8,128)(2,1)} async-done(((bf16[2352,768]{1,0:T(8,128)(2,1)}), bf16[1176,768]{1,0:T(8,128)(2,1)}) %reduce-scatter.5.cloned.1.call-update) | async-done | bytes 1806352 | tf_op jit(solution)/shard_map/reduce_scatter | solution.py:218
  303.2 46.8 %all-gather.7.cloned.1.call-done = bf16[2352,768]{1,0:T(8,128)(2,1)} async-done(((bf16[1176,768]{1,0:T(8,128)(2,1)}), bf16[2352,768]{1,0:T(8,128)(2,1)}) %all-gather.7.cloned.1.call-update) | async-done | bytes 3612688 | tf_op jit(solution)/shard_map/all_gather | solution.py:227
  350.1 12.2 %multiply_convert_fusion.1 = (bf16[2352,1536]{1,0:T(8,128)(2,1)}, f32[2352,1536]{1,0:T(8,128)}) fusion(f32[1536]{0:T(1024)S(1)} %copy-done.40, bf16[2352,768]{1,0:T(8,128)(2,1)} %all-gather.7.cloned.1.call-done, bf16[768,1536]{1,0:T(8,128)(2,1)S(1)} %copy-done), kind=kOutput, calls=%fused_computation.60 | convolution fusion | flops 5570740224 | bytes 27654144 | tf_op jit(solution)/shard_map/dot_general | solution.py:229
  362.3 39.9 %all-gather.9.cloned.1.call-done = bf16[2352,768]{1,0:T(8,128)(2,1)} async-done(((bf16[1176,768]{1,0:T(8,128)(2,1)}), bf16[2352,768]{1,0:T(8,128)(2,1)}) %all-gather.9.cloned.1.call-update) | async-done | bytes 3612688 | tf_op jit(solution)/shard_map/all_gather | solution.py:242
  402.2 13.4 %fusion.88 = (f32[1536]{0:T(1024)}, bf16[2352,1536]{1,0:T(8,128)(2,1)S(1)}) fusion(f32[2352,1536]{1,0:T(8,128)} %get-tuple-element.328, bf16[2352,768]{1,0:T(8,128)(2,1)} %all-gather.9.cloned.1.call-done, bf16[1536,768]{1,0:T(8,128)(2,1)} %param.34), kind=kOutput, calls=%fused_computation.152 | convolution fusion | flops 5588802048 | bytes 27654144 | tf_op jit(solution)/shard_map/dot_general | solution.py:68
  427.5 10.2 convolution_convert_fusion.1
  437.8 36.8 %reduce-scatter.9.cloned.1.call-done = bf16[1176,768]{1,0:T(8,128)(2,1)} async-done(((bf16[2352,768]{1,0:T(8,128)(2,1)}), bf16[1176,768]{1,0:T(8,128)(2,1)}) %reduce-scatter.9.cloned.1.call-update) | async-done | bytes 1806352 | tf_op jit(solution)/shard_map/reduce_scatter | solution.py:249
  479.3 46.5 %reduce-scatter.7.cloned.1.call-done = bf16[1176,768]{1,0:T(8,128)(2,1)} async-done(((bf16[2352,768]{1,0:T(8,128)(2,1)}), bf16[1176,768]{1,0:T(8,128)(2,1)}) %reduce-scatter.7.cloned.1.call-update) | async-done | bytes 1806352 | tf_op jit(solution)/shard_map/reduce_scatter | solution.py:232
  536.1 50.2 %all-gather.11.cloned.1.call-done = bf16[2352,768]{1,0:T(8,128)(2,1)} async-done(((bf16[1176,768]{1,0:T(8,128)(2,1)}), bf16[2352,768]{1,0:T(8,128)(2,1)}) %all-gather.11.cloned.1.call-update) | async-done | bytes 3612688 | tf_op jit(solution)/shard_map/all_gather | solution.py:261
  594.6 15.1 %reshape.257 = bf16[4,12,49,12,32]{2,1,0,4,3:T(8,128)(2,1)} reshape(bf16[2352,384]{0,1:T(8,128)(2,1)S(1)} %copy.113) | data formatting | bytes 3612672 | tf_op jit(solution)/shard_map/reshape | solution.py:161
  617.6 71.5 %while.30 = (s32[]{:T(128)}, f32[12,49,49]{1,2,0:T(8,128)S(1)}, f32[4,12,49,12,32]{2,4,3,1,0:T(8,128)}, bf16[4,12,49,12,32]{2,4,3,1,0:T(8,128)(2,1)}, f32[4,12,4...) while((s32[]{:T(128)}, f32[12,49,49]{1,2,0:T(8,128)S(1)}, ...), condition=%wide.region_16.17_spmd.clone, body=%wide.region_13.16_spmd.clone.sunk | while | flops 115260352 | bytes 69294632 | solution.py:152
  689.1 12.7 %copy.120 = bf16[4,12,49,12,32]{2,1,0,4,3:T(8,128)(2,1)} copy(f32[4,12,49,12,32]{2,4,3,1,0:T(8,128)} %get-tuple-element.127) | data formatting | bytes 5419008 | tf_op jit(solution)/shard_map/while | solution.py:152
  712.3 12.7 %copy.118 = bf16[4,12,49,12,32]{2,1,0,4,3:T(8,128)(2,1)} copy(f32[4,12,49,12,32]{2,4,3,1,0:T(8,128)} %get-tuple-element.125) | data formatting | bytes 5419008 | tf_op jit(solution)/shard_map/while | solution.py:152
  754.0 9.8 bitcast_convert_fusion
  763.9 11.7 %fusion.75 = f32[768,1536]{1,0:T(8,128)} fusion(bf16[2352,768]{1,0:T(8,128)(2,1)} %all-gather.7.cloned.1.call-done, bf16[2352,1536]{1,0:T(8,128)(2,1)} %copy-done.41), kind=kOutput, calls=%fused_computation.110 | convolution fusion | flops 5549064192 | bytes 15556608 | tf_op jit(solution)/shard_map/dot_general | solution.py:68
  775.7 10.3 fusion.90
  808.4 63.6 %all-reduce.1 = (f32[2,384]{1,0:T(2,128)}, f32[169,12]{0,1:T(8,128)}, f32[1536]{0:T(1024)}) all-reduce(f32[2,384]{1,0:T(2,128)S(1)} %pad_maximum_fusion, f32[169,12]{0,1:T(8,128)S(1)} %fusion.80, f32[1536]{0:T(1024)S(1)} %copy-done.28), channel_id=1, replica_groups=mesh['dp'=16,'tensor'=2] {'dp'}, use_global_device_ids=true, to_apply=%region_27.28 | all-reduce | flops 4332 | bytes 34656 | tf_op jit(solution)/shard_map/psum | solution.py:297
  875.6 39.0 %all-reduce = (f32[768]{0:T(1024)}, f32[768]{0:T(1024)}, f32[768]{0:T(1024)}, f32[768]{0:T(1024)}, f32[768]{0:T(1024)}, /*index=5*/f32[768]{0:T(1024)}) all-reduce(f32[768]{0:T(1024)S(1)} %get-tuple-element.250, f32[768]{0:T(1024)S(1)} %get-tuple-element.255, ...), channel_id=1, replica_groups=mesh['dp'=16,'tensor'=2] {'dp','tensor'}, use_global_device_ids=true, to_apply=%region_21.22 | all-reduce | flops 4608 | bytes 36864 | tf_op jit(solution)/shard_map/psum | solution.py:316
  919.1 156.9 %all-reduce.5.cloned.1.call-done = (f32[768,3,384]{2,0,1:T(8,128)}, f32[384,768]{1,0:T(8,128)}, f32[768,1536]{1,0:T(8,128)}, f32[1536,768]{1,0:T(8,128)}) async-done(((f32[768,3,384]{2,0,1:T(8,128)}, f32[384,768]{1,0:T(8,128)}, f32[768,1536]{1,0:T(8,128)}, f32[1536,768]{1,0:T(8,128)}), (f32[768,3,384]{2,0,1:T(8,128)}, f32[384,768]{1,0:T(8,128)}, f32[768,1536]{1,0:T(8,128)}, ...) | async-done | bytes 14155792 | tf_op jit(solution)/shard_map/psum | solution.py:297
  (312 shorter events, 346.4 us)
Async XLA Ops:
  7.2 342.9 %copy-start = (bf16[768,1536]{1,0:T(8,128)(2,1)S(1)}, bf16[768,1536]{1,0:T(8,128)(2,1)}, u32[]{:S(2)}) copy-start(bf16[768,1536]{1,0:T(8,128)(2,1)} %param.32) | copy-start | bytes 7077892
  7.2 59.9 %all-gather.5.cloned.1.call-start = ((), (), s32[]{:S(2)}) async-start(), calls=%async_computation.4 | async-start | bytes 5419008 | tf_op jit(solution)/shard_map/all_gather | solution.py:201
  14.0 279.2 %reduce-scatter.5.cloned.1.call-start = ((), (), s32[]{:S(2)}) async-start(), calls=%async_computation.5 | async-start | bytes 5419008 | tf_op jit(solution)/shard_map/reduce_scatter | solution.py:218
  14.7 59.8 %copy-start.26 = (s32[2401]{0:T(1024)}, s32[2401]{0:T(1024)S(1)}, u32[]{:S(2)}) copy-start(s32[2401]{0:T(1024)S(1)} %reshape.262) | copy-start | bytes 28816
  244.6 48.7 %copy-start.18 = (f32[768]{0:T(1024)S(1)}, f32[768]{0:T(1024)}, u32[]{:S(2)}) copy-start(f32[768]{0:T(1024)} %param.29) | copy-start | bytes 9220
  244.6 52.9 %copy-start.19 = (f32[768]{0:T(1024)S(1)}, f32[768]{0:T(1024)}, u32[]{:S(2)}) copy-start(f32[768]{0:T(1024)} %param.30) | copy-start | bytes 9220
  244.6 52.9 %copy-start.31 = (f32[768]{0:T(1024)S(1)}, f32[768]{0:T(1024)}, u32[]{:S(2)}) copy-start(f32[768]{0:T(1024)} %param.31) | copy-start | bytes 9220
  244.6 105.5 %all-gather.7.cloned.1.call-start = ((), (), s32[]{:S(2)}) async-start(), calls=%async_computation.6 | async-start | bytes 5419008 | tf_op jit(solution)/shard_map/all_gather | solution.py:227
  299.7 50.4 %copy-start.40 = (f32[1536]{0:T(1024)S(1)}, f32[1536]{0:T(1024)}, u32[]{:S(2)}) copy-start(f32[1536]{0:T(1024)} %param.33) | copy-start | bytes 18436
  299.7 102.5 %all-gather.9.cloned.1.call-start = ((), (), s32[]{:S(2)}) async-start(), calls=%async_computation.8 | async-start | bytes 5419008 | tf_op jit(solution)/shard_map/all_gather | solution.py:242
  303.2 171.4 %reduce-scatter.9.cloned.1.call-start = ((), (), s32[]{:S(2)}) async-start(), calls=%async_computation.9 | async-start | bytes 5419008 | tf_op jit(solution)/shard_map/reduce_scatter | solution.py:249
  425.9 100.0 %reduce-scatter.7.cloned.1.call-start = ((), (), s32[]{:S(2)}) async-start(), calls=%async_computation.7 | async-start | bytes 5419008 | tf_op jit(solution)/shard_map/reduce_scatter | solution.py:232
  437.8 88.1 %copy-start.30 = (f32[768]{0:T(1024)S(1)}, f32[768]{0:T(1024)}, u32[]{:S(2)}) copy-start(f32[768]{0:T(1024)} %param.35) | copy-start | bytes 9220
  437.8 148.5 %all-gather.11.cloned.1.call-start = ((), (), s32[]{:S(2)}) async-start(), calls=%async_computation.10 | async-start | bytes 5419008 | tf_op jit(solution)/shard_map/all_gather | solution.py:261
  536.0 336.0 %reduce-scatter.11.cloned.1.call-start = ((), (), s32[]{:S(2)}) async-start(), calls=%async_computation.11 | async-start | bytes 5419008 | tf_op jit(solution)/shard_map/reduce_scatter | solution.py:279
  763.9 312.1 %all-reduce.5.cloned.1.call-start = ((), (), s32[]{:S(2)}) async-start(), calls=%async_computation.12 | async-start | bytes 28311552 | tf_op jit(solution)/shard_map/psum | solution.py:297
  802.0 70.0 %copy-start.5 = (bf16[1176,768]{1,0:T(8,128)(2,1)S(1)}, bf16[1176,768]{1,0:T(8,128)(2,1)}, u32[]{:S(2)}) copy-start(bf16[1176,768]{1,0:T(8,128)(2,1)} %param.20) | copy-start | bytes 5419012
  802.0 70.0 %copy-start.15 = (f32[1176]{0:T(1024)S(1)}, f32[1176]{0:T(1024)}, u32[]{:S(2)}) copy-start(f32[1176]{0:T(1024)} %copy-done.14) | copy-start | bytes 14116
  802.0 70.0 %copy-start.17 = (f32[1176]{0:T(1024)S(1)}, f32[1176]{0:T(1024)}, u32[]{:S(2)}) copy-start(f32[1176]{0:T(1024)} %copy-done.16) | copy-start | bytes 14116
  802.0 70.0 %copy-start.21 = (f32[768]{0:T(1024)S(1)}, f32[768]{0:T(1024)}, u32[]{:S(2)}) copy-start(f32[768]{0:T(1024)} %param.23) | copy-start | bytes 9220
  806.9 68.7 %copy-start.22 = (f32[768]{0:T(1024)S(1)}, f32[768]{0:T(1024)}, u32[]{:S(2)}) copy-start(f32[768]{0:T(1024)} %get-tuple-element.248) | copy-start | bytes 9220
  806.9 68.7 %copy-start.23 = (f32[768]{0:T(1024)S(1)}, f32[768]{0:T(1024)}, u32[]{:S(2)}) copy-start(f32[768]{0:T(1024)} %get-tuple-element.254) | copy-start | bytes 9220
  806.9 68.7 %copy-start.24 = (f32[768]{0:T(1024)S(1)}, f32[768]{0:T(1024)}, u32[]{:S(2)}) copy-start(f32[768]{0:T(1024)} %get-tuple-element.315) | copy-start | bytes 9220
  806.9 68.7 %copy-start.25 = (f32[768]{0:T(1024)S(1)}, f32[768]{0:T(1024)}, u32[]{:S(2)}) copy-start(f32[768]{0:T(1024)} %get-tuple-element.324) | copy-start | bytes 9220
  (50 other events, 236.8 us)
Sparse Core Ops, SparseCore 0:
  14.1 52.8 all-gather.4
  244.7 48.5 reduce-scatter.4
  299.8 50.1 all-gather.6
  352.0 50.1 all-gather.8
  426.0 48.5 reduce-scatter.8
  477.3 48.5 reduce-scatter.6
  536.1 50.1 all-gather.10
  764.0 48.5 reduce-scatter.10
  818.3 257.6 all-reduce.4
where the time goes:
time: 1100 us; the launch traced here: 1090 us
  waiting for transfers between devices  473 us (43%)
  local copies, waits for them, and re-layouts  230 us (21%)
  matrix products  195 us (18%)
  blocking collectives  103 us (9%)
  other arithmetic  76.6 us (7%)
  between operations  14.6 us (1%)
    psum x1, waiting for transfers between devices, local(): lax.psum((qkv_weight_grad, query_value_bias_grad, relative_bias_grad, pro...  157 us
    dot_general x10, matrix products, product(): lax.dot_general(left, right, (((left_dim,), (right_dim,)), ((), ())), pre...  83.6 us
    psum x1, blocking collectives, local(): lax.psum((qkv_weight_grad, query_value_bias_grad, relative_bias_grad, pro...  63.6 us
    all_gather x1, waiting for transfers between devices, local(): branch_in = lax.all_gather(residual_low, 'tensor', axis=0, tiled=True)  50.2 us
    reduce_scatter x1, waiting for transfers between devices, local(): lax.psum_scatter(slice_product(attended, proj_local, 0).astype(jnp.bfloat...  48.6 us
    all_gather x1, waiting for transfers between devices, local(): attn_in = lax.all_gather(normed1_low, 'tensor', axis=0, tiled=True)  47.2 us
    all_gather x1, waiting for transfers between devices, local(): mlp_in = lax.all_gather(normed2_low, 'tensor', axis=0, tiled=True)  46.8 us
    reduce_scatter x1, waiting for transfers between devices, local(): lax.psum_scatter(slice_product(activation_low, down_local, 0).astype(jnp....  46.5 us
  transfers between devices with their start and end apart: 9, of which 8 were waited for; matrix products, arithmetic and copies ran while one was open for 8% of the time, Pallas kernels for 0%

commit v1 on v0

v1 whole, which is shorter than its diff:
```python
import functools
import jax, jax.numpy as jnp
from jax import lax
from jax.experimental import pallas as pl
from jax.experimental.pallas import tpu as pltpu
from jax.sharding import PartitionSpec as P

WIN = 7
PATCHES = WIN * WIN
SLOT = 64
LANES = 128
HEAD_DIM = 32
PER_GROUP = LANES // HEAD_DIM
SPREAD = PER_GROUP * SLOT
BLOCK = 8
ROWS = BLOCK * PATCHES
SCALE = HEAD_DIM ** -0.5


def dot_last(left, right):
    return lax.dot_general(left, right, (((1,), (1,)), ((), ())), preferred_element_type=jnp.float32)


def dot_first(left, right):
    return lax.dot_general(left, right, (((0,), (0,)), ((), ())), preferred_element_type=jnp.float32)


def dot_plain(left, right):
    return jnp.dot(left, right, preferred_element_type=jnp.float32)


def head_lanes(rows):
    lane = lax.broadcasted_iota(jnp.int32, (rows, LANES), 1) // HEAD_DIM
    return [lane == head for head in range(PER_GROUP)]


def spread_heads(rows, masks):
    zero = jnp.zeros_like(rows)
    return jnp.concatenate([jnp.where(mask, rows, zero) for mask in masks], axis=0)


def gather_heads(full, masks):
    out = jnp.zeros((SLOT, LANES), jnp.float32)
    for head, mask in enumerate(masks):
        out = jnp.where(mask, full[head * SLOT : (head + 1) * SLOT], out)
    return out


def attend_kernel(groups, x_ref, w_ref, shift_ref, bias_ref, mask_ref, att_ref, qkv_ref, prob_ref, mix, held, flat):
    width = groups * LANES
    mix[ROWS:, :] = jnp.zeros((mix.shape[0] - ROWS, 3 * width), jnp.float32)
    for part in range(3):
        cols = pl.ds(part * width, width)
        mix[:ROWS, cols] = dot_plain(x_ref[...], w_ref[:, cols]) + shift_ref[:, cols]
    for window in range(BLOCK):
        qkv_ref[window] = mix[pl.ds(window * PATCHES, SLOT), :].astype(jnp.bfloat16)
    masks = head_lanes(SLOT)
    low_half = lax.broadcasted_iota(jnp.int32, (SLOT, LANES), 1) < SLOT
    ones = (
        lax.broadcasted_iota(jnp.int32, (SPREAD, SPREAD), 0) // SLOT
        == lax.broadcasted_iota(jnp.int32, (SPREAD, SPREAD), 1) // SLOT
    ).astype(jnp.float32).astype(jnp.bfloat16)
    least = jnp.float32(-3e38)

    def segment_max(scores):
        parts = []
        for half in range(SPREAD // LANES):
            piece = scores[:, half * LANES : (half + 1) * LANES]
            first = jnp.max(jnp.where(low_half, piece, least), axis=-1, keepdims=True)
            second = jnp.max(jnp.where(low_half, least, piece), axis=-1, keepdims=True)
            parts.append(jnp.where(low_half, first, second))
        return jnp.concatenate(parts, axis=1)

    def one_window(window, carry):
        for group in range(groups):
            lanes = pl.ds(group * LANES, LANES)
            query = qkv_ref[window, :, lanes]
            key = spread_heads(qkv_ref[window, :, pl.ds(width + group * LANES, LANES)], masks)
            value = spread_heads(qkv_ref[window, :, pl.ds(2 * width + group * LANES, LANES)], masks)
            scores = dot_last(query, key) * SCALE + bias_ref[group] + mask_ref[window]
            weights = jnp.exp(scores - segment_max(scores))
            total = dot_plain(weights.astype(jnp.bfloat16), ones)
            probs = (weights / total).astype(jnp.bfloat16)
            prob_ref[window, group] = probs
            held[window, :, lanes] = dot_plain(probs, value)
        return carry

    lax.fori_loop(0, BLOCK, one_window, 0)
    for window in range(BLOCK):
        flat[pl.ds(window * PATCHES, SLOT), :] = held[window]
    att_ref[...] = flat[:ROWS, :].astype(jnp.bfloat16)


TAIL = (BLOCK - 1) * PATCHES + SLOT
TAIL = (TAIL + 7) // 8 * 8


def attend(normed, weight, shift, bias, mask):
    windows = mask.shape[0]
    width = weight.shape[1] // 3
    groups = width // LANES
    fixed = lambda shape: pl.BlockSpec(shape, lambda i: (0,) * len(shape))
    return pl.pallas_call(
        functools.partial(attend_kernel, groups),
        grid=(windows // BLOCK,),
        in_specs=[
            pl.BlockSpec((ROWS, normed.shape[1]), lambda i: (i, 0)),
            fixed(weight.shape),
            fixed(shift.shape),
            fixed(bias.shape),
            pl.BlockSpec((BLOCK, 1, SPREAD), lambda i: (i, 0, 0)),
        ],
        out_specs=[
            pl.BlockSpec((ROWS, width), lambda i: (i, 0)),
            pl.BlockSpec((BLOCK, SLOT, 3 * width), lambda i: (i, 0, 0)),
            pl.BlockSpec((BLOCK, groups, SLOT, SPREAD), lambda i: (i, 0, 0, 0)),
        ],
        out_shape=[
            jax.ShapeDtypeStruct((windows * PATCHES, width), jnp.bfloat16),
            jax.ShapeDtypeStruct((windows, SLOT, 3 * width), jnp.bfloat16),
            jax.ShapeDtypeStruct((windows, groups, SLOT, SPREAD), jnp.bfloat16),
        ],
        scratch_shapes=[
            pltpu.VMEM((TAIL, 3 * width), jnp.float32),
            pltpu.VMEM((BLOCK, SLOT, width), jnp.float32),
            pltpu.VMEM((TAIL, width), jnp.float32),
        ],
        cost_estimate=pl.CostEstimate(
            flops=2 * normed.size * weight.shape[1] + 8 * windows * groups * SLOT * SPREAD * SPREAD,
            bytes_accessed=2 * (normed.size + weight.size + windows * SLOT * (4 * width + groups * SPREAD)),
            transcendentals=windows * groups * SLOT * SPREAD,
        ),
    )(normed, weight, shift, bias, mask)


def attend_grad_kernel(groups, grad_ref, att_ref, qkv_ref, prob_ref, out_ref, table_ref, sum_ref, rise, pair, held, flat):
    width = groups * LANES
    step = pl.program_id(0)

    @pl.when(step == 0)
    def _():
        table_ref[...] = jnp.zeros_like(table_ref)
        sum_ref[...] = jnp.zeros_like(sum_ref)

    masks = head_lanes(SLOT)
    real = lax.broadcasted_iota(jnp.int32, (SLOT, LANES), 0) < PATCHES
    rise[ROWS:, :] = jnp.zeros((rise.shape[0] - ROWS, 2 * width), jnp.float32)
    for group in range(groups):
        lanes = pl.ds(group * LANES, LANES)
        grad = grad_ref[:, lanes].astype(jnp.float32)
        rise[:ROWS, pl.ds(2 * group * LANES, LANES)] = grad
        rise[:ROWS, pl.ds((2 * group + 1) * LANES, LANES)] = grad * att_ref[:, lanes].astype(jnp.float32)
    for window in range(BLOCK):
        for group in range(2 * groups):
            lanes = pl.ds(group * LANES, LANES)
            pair[window, :, lanes] = jnp.where(real, rise[pl.ds(window * PATCHES, SLOT), lanes], 0.0).astype(jnp.bfloat16)
    minus = spread_heads(jnp.full((SLOT, LANES), -1.0, jnp.bfloat16), masks)

    def one_window(window, carry):
        for group in range(groups):
            spot = [pl.ds(part * width + group * LANES, LANES) for part in range(3)]
            query = qkv_ref[window, :, spot[0]]
            key = spread_heads(qkv_ref[window, :, spot[1]], masks)
            value = spread_heads(qkv_ref[window, :, spot[2]], masks)
            both = pair[window, :, pl.ds(2 * group * LANES, 2 * LANES)]
            probs = prob_ref[window, group]
            lift = dot_last(both, jnp.concatenate([value, minus], axis=1))
            score_grad = (probs.astype(jnp.float32) * lift).astype(jnp.bfloat16)
            table_ref[group] += score_grad.astype(jnp.float32)
            held[window, :, spot[0]] = dot_plain(score_grad, key) * SCALE
            held[window, :, spot[1]] = gather_heads(dot_first(score_grad, query), masks) * SCALE
            held[window, :, spot[2]] = gather_heads(dot_first(probs, both[:, :LANES]), masks)
        return carry

    lax.fori_loop(0, BLOCK, one_window, 0)
    for window in range(BLOCK):
        flat[pl.ds(window * PATCHES, SLOT), :] = held[window]
    out_ref[...] = flat[:ROWS, :].astype(jnp.bfloat16)
    sum_ref[...] += jnp.sum(flat[:ROWS, :].reshape(ROWS // 8, 8, 3 * width), axis=0)


def attend_grad(grad, attended, qkv, probs):
    windows, groups = probs.shape[:2]
    width = groups * LANES
    rows = lambda cols: pl.BlockSpec((ROWS, cols), lambda i: (i, 0))
    return pl.pallas_call(
        functools.partial(attend_grad_kernel, groups),
        grid=(windows // BLOCK,),
        in_specs=[
            rows(width),
            rows(width),
            pl.BlockSpec((BLOCK, SLOT, 3 * width), lambda i: (i, 0, 0)),
            pl.BlockSpec((BLOCK, groups, SLOT, SPREAD), lambda i: (i, 0, 0, 0)),
        ],
        out_specs=[
            rows(3 * width),
            pl.BlockSpec((groups, SLOT, SPREAD), lambda i: (0, 0, 0)),
            pl.BlockSpec((8, 3 * width), lambda i: (0, 0)),
        ],
        out_shape=[
            jax.ShapeDtypeStruct((windows * PATCHES, 3 * width), jnp.bfloat16),
            jax.ShapeDtypeStruct((groups, SLOT, SPREAD), jnp.float32),
            jax.ShapeDtypeStruct((8, 3 * width), jnp.float32),
        ],
        scratch_shapes=[
            pltpu.VMEM((TAIL, 2 * width), jnp.float32),
            pltpu.VMEM((BLOCK, SLOT, 2 * width), jnp.bfloat16),
            pltpu.VMEM((BLOCK, SLOT, 3 * width), jnp.float32),
            pltpu.VMEM((TAIL, 3 * width), jnp.float32),
        ],
        cost_estimate=pl.CostEstimate(
            flops=16 * windows * groups * SLOT * SPREAD * SPREAD,
            bytes_accessed=2 * windows * SLOT * (8 * width + groups * SPREAD),
            transcendentals=0,
        ),
    )(grad, attended, qkv, probs)


norm_epsilon = 1e-05
masked_score = -1e30
highest = lax.Precision.HIGHEST
low = jnp.bfloat16


def window_masks(window_extent):
    places = jnp.arange(PATCHES, dtype=jnp.int32)
    rows_at = places // WIN
    cols_at = places % WIN
    return (rows_at[None, :] < window_extent[:, 0:1]) & (cols_at[None, :] < window_extent[:, 1:2])


def relative_onehot():
    places = jnp.arange(PATCHES, dtype=jnp.int32)
    rows_at = places // WIN
    cols_at = places % WIN
    index = (
        (rows_at[:, None] - rows_at[None, :] + WIN - 1) * (2 * WIN - 1)
        + cols_at[:, None]
        - cols_at[None, :]
        + WIN
        - 1
    )
    slots = jnp.arange((2 * WIN - 1) ** 2, dtype=jnp.int32)
    return (index.reshape(-1)[:, None] == slots[None, :]).astype(jnp.float32)


def spread_bias(onehot, table):
    heads = table.shape[1]
    flat = jnp.dot(onehot, table, precision=highest, preferred_element_type=jnp.float32)
    square = flat.T.reshape(heads, PATCHES, PATCHES)
    rest = SLOT - PATCHES
    square = jnp.pad(square, ((0, 0), (0, rest), (0, 0)))
    square = jnp.pad(square, ((0, 0), (0, 0), (0, rest)), constant_values=masked_score)
    square = square.reshape(heads // PER_GROUP, PER_GROUP, SLOT, SLOT)
    return square.transpose(0, 2, 1, 3).reshape(heads // PER_GROUP, SLOT, SPREAD)


def collect_bias(onehot, grads):
    groups = grads.shape[0]
    square = grads.reshape(groups, SLOT, PER_GROUP, SLOT)[:, :PATCHES, :, :PATCHES]
    square = square.transpose(0, 2, 1, 3).reshape(groups * PER_GROUP, PATCHES * PATCHES)
    return lax.dot_general(
        onehot, square, (((0,), (1,)), ((), ())), precision=highest, preferred_element_type=jnp.float32
    )


def norm_forward(values, gain, shift):
    center = values - jnp.mean(values, axis=-1, keepdims=True)
    inverse = lax.rsqrt(jnp.mean(center * center, axis=-1, keepdims=True) + norm_epsilon)
    unit = center * inverse
    return (unit * gain + shift, unit, inverse)


def norm_backward(normed_grad, unit, inverse, gain):
    unit_grad = normed_grad * gain
    inputs_grad = inverse * (
        unit_grad
        - jnp.mean(unit_grad, axis=-1, keepdims=True)
        - unit * jnp.mean(unit_grad * unit, axis=-1, keepdims=True)
    )
    return (inputs_grad, jnp.sum(normed_grad * unit, axis=0), jnp.sum(normed_grad, axis=0))


def gelu_parts(hidden):
    cdf = 0.5 * (1.0 + lax.erf(hidden * 0.7071067811865476))
    slope = cdf + hidden * jnp.exp(-0.5 * hidden * hidden) * 0.3989422804014327
    return (hidden * cdf, slope)


def add_low(first, second):
    return (first.astype(jnp.float32) + second.astype(jnp.float32)).astype(low)


class Links:
    def __init__(self):
        self.count = lax.axis_size("dp")
        self.me = lax.axis_index("dp")
        self.rest = []
        bit = 4
        while bit < self.count:
            self.rest.append(bit)
            bit *= 2

    def hop(self, values, bit):
        return lax.ppermute(values, "dp", [(i, i ^ bit) for i in range(self.count)])

    def across(self, values):
        return lax.ppermute(values, "tensor", [(0, 1), (1, 0)])

    def side(self, bit):
        return (self.me // bit) % 2

    def fetch(self, weight):
        part = weight.shape[0] // 4
        place = lambda bit: ((self.me % 4) ^ bit) * part
        mine = lax.dynamic_slice_in_dim(weight, place(0), part, 0)
        first = self.across(mine)
        second = self.hop(first, 2)
        out = jnp.zeros_like(weight)
        pieces = ((first, 0), (second, 2), (self.hop(first, 1), 1), (self.hop(second, 1), 3))
        for piece, bit in pieces:
            out = lax.dynamic_update_slice_in_dim(out, piece, place(bit), 0)
        return out

    def halve(self, values, bit):
        part = values.shape[0] // 2
        side = self.side(bit)
        keep = lax.dynamic_slice_in_dim(values, side * part, part, 0)
        give = lax.dynamic_slice_in_dim(values, (1 - side) * part, part, 0)
        return add_low(keep, self.hop(give, bit))

    def join(self, values, bit):
        other = self.hop(values, bit)
        first = self.side(bit) == 0
        return jnp.concatenate([jnp.where(first, values, other), jnp.where(first, other, values)], axis=0)

    def share(self, other):
        return self.across(self.halve(other, 1))

    def reduce(self, own, arrived):
        values = self.halve(add_low(self.halve(own, 1), arrived), 2)
        for bit in self.rest:
            values = self.halve(values, bit)
        for bit in reversed(self.rest):
            values = self.join(values, bit)
        part = values.shape[0]
        place = lambda core, line: ((self.side(1) ^ core) * 2 + (self.side(2) ^ line)) * part
        second = self.hop(values, 2)
        out = jnp.zeros(own.shape, jnp.float32)
        pieces = ((values, 0, 0), (second, 0, 1), (self.hop(values, 1), 1, 0), (self.hop(second, 1), 1, 1))
        for piece, core, line in pieces:
            out = lax.dynamic_update_slice_in_dim(out, piece.astype(jnp.float32), place(core, line), 0)
        return out

    def total(self, values):
        for bit in [1, 2] + self.rest:
            values = values + self.hop(values, bit)
        return values


def pack(items):
    flat = jnp.concatenate([item.reshape(-1) for item in items])
    return jnp.pad(flat, (0, -flat.shape[0] % 1024)).reshape(-1, LANES)


def unpack(packed, shapes):
    flat, items, start = packed.reshape(-1), [], 0
    for shape in shapes:
        size = 1
        for extent in shape:
            size *= extent
        items.append(flat[start : start + size].reshape(shape))
        start += size
    return items


def local(
    tokens,
    cotangent,
    window_extent,
    norm1_gain,
    norm1_shift,
    qkv_weight,
    query_value_bias,
    relative_bias,
    proj_weight,
    proj_bias,
    norm2_gain,
    norm2_shift,
    up_weight,
    up_bias,
    down_weight,
    down_bias,
):
    width = tokens.shape[1]
    links = Links()
    key_mask = window_masks(window_extent)
    own_windows = key_mask.shape[0] // lax.axis_size("tensor")
    own_mask = lax.dynamic_slice_in_dim(
        key_mask, lax.axis_index("tensor") * own_windows, own_windows, 0
    )
    row_mask = own_mask.reshape(-1, 1).astype(jnp.float32)
    lane_mask = jnp.pad(own_mask, ((0, 0), (0, SLOT - PATCHES)), constant_values=True)
    lane_mask = jnp.where(jnp.tile(lane_mask, (1, PER_GROUP)), 0.0, masked_score)[:, None, :]
    onehot = relative_onehot()
    part_width = qkv_weight.shape[2]
    small_shapes = [query_value_bias.shape, relative_bias.shape, up_bias.shape]
    own_small = [query_value_bias, relative_bias, up_bias]
    other_small = unpack(links.across(pack(own_small)), small_shapes)
    qkv_own = qkv_weight.reshape(width, 3 * part_width)
    qkv_both = [qkv_own, links.fetch(qkv_own)]
    proj_both = [proj_weight, links.fetch(proj_weight)]
    up_both = [up_weight, links.fetch(up_weight)]
    down_both = [down_weight, links.fetch(down_weight)]
    shift_both, bias_both, up_bias_both = [], [], []
    for pair_bias, table, hidden_bias in (own_small, other_small):
        shift = jnp.concatenate([pair_bias[0], jnp.zeros_like(pair_bias[0]), pair_bias[1]])
        shift_both.append(shift[None])
        bias_both.append(spread_bias(onehot, table))
        up_bias_both.append(hidden_bias)

    inputs = tokens.astype(jnp.float32)
    normed1, unit1, inverse1 = norm_forward(inputs, norm1_gain, norm1_shift)
    normed1_low = normed1.astype(low)
    heads = [
        attend(normed1_low, qkv_both[side], shift_both[side], bias_both[side], lane_mask)
        for side in (0, 1)
    ]
    branch = dot_plain(heads[0][0], proj_both[0]) + dot_plain(heads[1][0], proj_both[1])
    residual = inputs + branch + proj_bias
    normed2, unit2, inverse2 = norm_forward(residual, norm2_gain, norm2_shift)
    normed2_low = normed2.astype(low)
    activations, slopes = [], []
    for side in (0, 1):
        activation, slope = gelu_parts(dot_plain(normed2_low, up_both[side]) + up_bias_both[side])
        activations.append(activation.astype(low))
        slopes.append(slope)
    down = dot_plain(activations[0], down_both[0]) + dot_plain(activations[1], down_both[1])
    block_out = (row_mask * (residual + down + down_bias)).astype(low)

    out_grad = row_mask * cotangent.astype(jnp.float32)
    down_bias_grad = jnp.sum(out_grad, axis=0)
    out_low = out_grad.astype(low)
    shared = {}
    down_grads, up_grads, up_bias_grads, hidden_lows = {}, {}, {}, {}
    for side in (1, 0):
        down_grads[side] = dot_first(activations[side], out_low).astype(low)
        hidden_grad = dot_last(out_low, down_both[side]) * slopes[side]
        up_bias_grads[side] = jnp.sum(hidden_grad, axis=0)
        hidden_lows[side] = hidden_grad.astype(low)
        up_grads[side] = dot_first(normed2_low, hidden_lows[side]).astype(low)
        if side == 1:
            shared["down"] = links.share(down_grads[1])
            shared["up"] = links.share(up_grads[1])
    down_weight_grad = links.reduce(down_grads[0], shared["down"])
    up_weight_grad = links.reduce(up_grads[0], shared["up"])
    normed2_grad = dot_last(hidden_lows[0], up_both[0]) + dot_last(hidden_lows[1], up_both[1])
    residual_part, norm2_gain_grad, norm2_shift_grad = norm_backward(
        normed2_grad, unit2, inverse2, norm2_gain
    )
    residual_grad = out_grad + residual_part
    proj_bias_grad = jnp.sum(residual_grad, axis=0)
    residual_low = residual_grad.astype(low)
    proj_grads = [dot_first(heads[side][0], residual_low).astype(low) for side in (0, 1)]
    proj_weight_grad = links.reduce(proj_grads[0], links.share(proj_grads[1]))
    mixed_grads, table_grads, pair_grads, qkv_grads = {}, {}, {}, {}
    for side in (1, 0):
        attended_grad = dot_last(residual_low, proj_both[side]).astype(low)
        attended, qkv, probs = heads[side]
        mixed_grads[side], table, sums = attend_grad(attended_grad, attended, qkv, probs)
        table_grads[side] = collect_bias(onehot, table)
        sums = jnp.sum(sums, axis=0).reshape(3, part_width)
        pair_grads[side] = jnp.stack([sums[0], sums[2]])
        qkv_grads[side] = dot_first(normed1_low, mixed_grads[side]).astype(low)
        if side == 1:
            shared["qkv"] = links.share(qkv_grads[1])
    qkv_weight_grad = links.reduce(qkv_grads[0], shared["qkv"]).reshape(width, 3, part_width)
    normed1_grad = dot_last(mixed_grads[0], qkv_both[0]) + dot_last(mixed_grads[1], qkv_both[1])
    tokens_part, norm1_gain_grad, norm1_shift_grad = norm_backward(
        normed1_grad, unit1, inverse1, norm1_gain
    )
    tokens_grad = residual_grad + tokens_part

    everywhere = [
        norm1_gain_grad,
        norm1_shift_grad,
        proj_bias_grad,
        norm2_gain_grad,
        norm2_shift_grad,
        down_bias_grad,
    ]
    own_part = pack([pair_grads[0], table_grads[0], up_bias_grads[0]])
    other_part = pack([pair_grads[1], table_grads[1], up_bias_grads[1]])
    both_part = pack(everywhere)
    arrived = links.across(jnp.concatenate([other_part, both_part], axis=0))
    sums = links.total(jnp.concatenate([own_part, both_part], axis=0) + arrived)
    query_value_bias_grad, relative_bias_grad, up_bias_grad = unpack(
        sums[: own_part.shape[0]], small_shapes
    )
    everywhere = unpack(sums[own_part.shape[0] :], [(width,)] * len(everywhere))
    (
        norm1_gain_grad,
        norm1_shift_grad,
        proj_bias_grad,
        norm2_gain_grad,
        norm2_shift_grad,
        down_bias_grad,
    ) = everywhere
    return (
        block_out,
        tokens_grad,
        norm1_gain_grad,
        norm1_shift_grad,
        qkv_weight_grad,
        query_value_bias_grad,
        relative_bias_grad,
        proj_weight_grad,
        proj_bias_grad,
        norm2_gain_grad,
        norm2_shift_grad,
        up_weight_grad,
        up_bias_grad,
        down_weight_grad,
        down_bias_grad,
    )


def solution(mesh):
    return jax.shard_map(
        local,
        mesh=mesh,
        in_specs=(
            P(("dp", "tensor"), None),
            P(("dp", "tensor"), None),
            P("dp", None),
            P(),
            P(),
            P(None, None, "tensor"),
            P(None, "tensor"),
            P(None, "tensor"),
            P("tensor", None),
            P(),
            P(),
            P(),
            P(None, "tensor"),
            P("tensor"),
            P("tensor", None),
            P(),
        ),
        out_specs=(
            P(("dp", "tensor"), None),
            P(("dp", "tensor"), None),
            P(),
            P(),
            P(None, None, "tensor"),
            P(None, "tensor"),
            P(None, "tensor"),
            P("tensor", None),
            P(),
            P(),
            P(),
            P(None, "tensor"),
            P("tensor"),
            P("tensor", None),
            P(),
        ),
        check_vma=False,
    )
```

time: 1100 us -> 571 us (0.52)
  waiting for transfers between devices: 473 us -> 144 us
  local copies, waits for them, and re-layouts: 230 us -> 111 us
  Pallas kernels: 0 us -> 108 us
  blocking collectives: 103 us -> 0 us
  matrix products: 195 us -> 116 us
  starting transfers between devices: 0.37 us -> 53.1 us
  other arithmetic: 76.6 us -> 28.4 us
  between operations: 14.6 us -> 2.77 us
    all_gather x4 -> x0, waiting for transfers between devices: 184 us -> none  [the longest x1 50.2 us: local(): branch_in = lax.all_gather(residual_low, 'tensor', axis=0, tiled=True)]
    psum x1 -> x0, waiting for transfers between devices: 157 us -> none  [local(): lax.psum((qkv_weight_grad, query_value_bias_grad, relative_bias_grad, pro...]
    ppermute x0 -> x66, waiting for transfers between devices: none -> 144 us  [the longest x56 99 us: hop(): return lax.ppermute(values, 'dp', [(i, i ^ bit) for i in range(self.count)])]
    reduce_scatter x4 -> x0, waiting for transfers between devices: 132 us -> none  [the longest x1 48.6 us: local(): lax.psum_scatter(slice_product(attended, proj_local, 0).astype(jnp.bfloat...]
    pallas_call x0 -> x4, Pallas kernels: none -> 108 us  [the longest x2 63.1 us: attend(): pl.pallas_call(functools.partial(attend_kernel, groups), grid=(windows //...]
    psum x2 -> x0, blocking collectives: 103 us -> none  [the longest x1 63.6 us: local(): lax.psum((qkv_weight_grad, query_value_bias_grad, relative_bias_grad, pro...]
    dot_general x42 -> x26, matrix products: 195 us -> 116 us  [the longest x8 43.1 us: dot_last(): lax.dot_general(left, right, (((1,), (1,)), ((), ())), preferred_element_...]
    while x48 -> x0, local copies, waits for them, and re-layouts: 66.2 us -> none  [the longest x4 33.9 us: attention_backward(): lax.scan(one_block, start, (queries.reshape(shape), key_rows.reshape(shap...]
  transfers between devices with their start and end apart: 9 -> 66, of which waited for: 8 -> 25; matrix products, arithmetic and copies ran while one was open for 8% -> 43% of each run, Pallas kernels for 0% -> 19%
where the time goes in v1:
time: 571 us; the launch traced here: 564 us
  waiting for transfers between devices  144 us (25%)
  matrix products  116 us (20%)
  local copies, waits for them, and re-layouts  111 us (19%)
  Pallas kernels  108 us (19%)
  starting transfers between devices  53.1 us (9%)
  other arithmetic  28.4 us (5%)
    ppermute x56, waiting for transfers between devices, hop(): return lax.ppermute(values, 'dp', [(i, i ^ bit) for i in range(self.count)])  99 us
    pallas_call x2, Pallas kernels, attend(): pl.pallas_call(functools.partial(attend_kernel, groups), grid=(windows //...  63.1 us
    ppermute x10, waiting for transfers between devices, across(): return lax.ppermute(values, 'tensor', [(0, 1), (1, 0)])  45.4 us
    pallas_call x2, Pallas kernels, attend_grad(): pl.pallas_call(functools.partial(attend_grad_kernel, groups), grid=(windo...  44.7 us
    dot_general x8, matrix products, dot_last(): lax.dot_general(left, right, (((1,), (1,)), ((), ())), preferred_element_...  43.1 us
    ppermute x56, starting transfers between devices, hop(): return lax.ppermute(values, 'dp', [(i, i ^ bit) for i in range(self.count)])  40.2 us
    dot_general x8, matrix products, dot_first(): lax.dot_general(left, right, (((0,), (0,)), ((), ())), preferred_element_...  33.3 us
    dot_general x6, matrix products, dot_plain(): return jnp.dot(left, right, preferred_element_type=jnp.float32)  30.1 us
  transfers between devices with their start and end apart: 66, of which 25 were waited for; matrix products, arithmetic and copies ran while one was open for 43% of the time, Pallas kernels for 19%

profile of v1, /device:TPU:0, one launch (start us, length us, event | category | flops | bytes accessed | tf_op | source)
XLA Modules:
  0.0 563.7 jit_solution(15320422757735143795)
XLA Ops:
  37.1 31.6 %shard_map.271 = (bf16[1176,384]{1,0:T(8,128)(2,1)}, bf16[24,64,1152]{2,1,0:T(8,128)(2,1)}, bf16[24,3,64,256]{3,2,1,0:T(8,128)(2,1)}) custom-call(bf16[1176,768]{1,0:T(8,128)(2,1)} %fusion.19.x_ref, bf16[768,1152]{1,0:T(8,128)(2,1)} %copy.35.w_ref, f32[1,1152]{1,0:T(1,128)} %broadcast_in_dim.28.shift_ref, f32[3,64,256]{2,1,0:T(8,128)} %reshape.308.bias_ref, ...), custom_call_target="tpu_custom_call" | custom-call | flops 4496818176 | bytes 10653696 | tf_op jit(solution)/shard_map/pallas_call | solution.py:103
  98.2 9.9 %collective-permute-done.10 = bf16[192,1536]{1,0:T(8,128)(2,1)} collective-permute-done((bf16[192,1536]{1,0:T(8,128)(2,1)}, bf16[192,1536]{1,0:T(8,128)(2,1)}, u32[]{:S(2)}, u32[]{:S(2)}) %collective-permute-start.10) | collective-permute-done | bytes 589856 | tf_op jit(solution)/shard_map/ppermute | solution.py:305
  108.1 12.1 %collective-permute-done.14 = bf16[384,768]{1,0:T(8,128)(2,1)} collective-permute-done((bf16[384,768]{1,0:T(8,128)(2,1)}, bf16[384,768]{1,0:T(8,128)(2,1)}, u32[]{:S(2)}, u32[]{:S(2)}) %collective-permute-start.14) | collective-permute-done | bytes 589856 | tf_op jit(solution)/shard_map/ppermute | solution.py:305
  126.6 31.5 %shard_map.272 = (bf16[1176,384]{1,0:T(8,128)(2,1)}, bf16[24,64,1152]{2,1,0:T(8,128)(2,1)}, bf16[24,3,64,256]{3,2,1,0:T(8,128)(2,1)}) custom-call(bf16[1176,768]{1,0:T(8,128)(2,1)} %fusion.19.x_ref, bf16[768,1152]{1,0:T(8,128)(2,1)} %constant_dynamic-update-slice_fusion.12.w_ref, f32[1,1152]{1,0:T(1,128)} %broadcast_in_dim.32.shift_ref, ...), custom_call_target="tpu_custom_call" | custom-call | flops 4496818176 | bytes 10653696 | tf_op jit(solution)/shard_map/pallas_call | solution.py:103
  177.4 7.7 %fusion.62 = (f32[1536]{0:T(1024)}, bf16[1176,1536]{1,0:T(8,128)(2,1)S(1)}) fusion(f32[1176,1536]{1,0:T(8,128)S(1)} %get-tuple-element.107, bf16[1536,768]{1,0:T(8,128)(2,1)S(1)} %copy-done.33, bf16[1176,768]{1,0:T(8,128)(2,1)S(1)} %copy-done.22, f32[1176]{0:T(1024)S(1)} %copy-done.38), kind=kOutput, calls=%fused_computation.243 | convolution fusion | flops 2797109760 | bytes 15014496 | tf_op jit(solution)/shard_map/dot_general | solution.py:21
  197.9 6.3 %multiply_convert_fusion = (bf16[1176,1536]{1,0:T(8,128)(2,1)}, f32[1176,1536]{1,0:T(8,128)S(1)}) fusion(f32[1536]{0:T(1024)S(1)} %copy-done.54, bf16[1176,768]{1,0:T(8,128)(2,1)S(1)} %add_convert_fusion, bf16[768,1536]{1,0:T(8,128)(2,1)} %constant_dynamic-update-slice_fusion.4), kind=kOutput, calls=%fused_computation.14 | convolution fusion | flops 2785370112 | bytes 15009792 | tf_op jit(solution)/shard_map/dot_general | solution.py:29
  206.1 7.5 %fusion.61 = (f32[1536]{0:T(1024)}, bf16[1176,1536]{1,0:T(8,128)(2,1)S(1)}) fusion(f32[1176,1536]{1,0:T(8,128)S(1)} %get-tuple-element.109, bf16[1536,768]{1,0:T(8,128)(2,1)} %constant_dynamic-update-slice_fusion, bf16[1176,768]{1,0:T(8,128)(2,1)S(1)} %copy-done.22, f32[1176]{0:T(1024)S(1)} %copy-done.38), kind=kOutput, calls=%fused_computation.242 | convolution fusion | flops 2797109760 | bytes 15014496 | tf_op jit(solution)/shard_map/dot_general | solution.py:21
  213.6 7.2 %multiply_reduce_fusion = (f32[768]{0:T(1024)S(1)}, f32[1176]{0:T(1024)S(1)}, f32[1176]{0:T(1024)S(1)}, f32[768]{0:T(1024)S(1)}, f32[1176,768]{1,0:T(8,128)S(1)}) fusion(f32[1176,768]{1,0:T(8,128)S(1)} %get-tuple-element.105, f32[1176]{0:T(1024)S(1)} %add_rsqrt_fusion, f32[1176]{0:T(1024)S(1)} %broadcast_multiply_fusion.4, f32[768]{0:T(1024)S(1)} %copy-done.45, ...), kind=kOutput, calls=%fused_computation.43 | convolution fusion | flops 2783559680 | bytes 16838016 | tf_op jit(solution)/shard_map/dot_general | solution.py:21
  228.6 22.2 %shard_map.273 = (bf16[1176,1152]{1,0:T(8,128)(2,1)}, f32[3,64,256]{2,1,0:T(8,128)}, f32[8,1152]{1,0:T(8,128)}) custom-call(bf16[1176,384]{1,0:T(8,128)(2,1)} %convolution_convert_fusion.7.grad_ref, bf16[1176,384]{1,0:T(8,128)(2,1)} %get-tuple-element.27.att_ref, bf16[24,64,1152]{2,1,0:T(8,128)(2,1)} %get-tuple-element.29.qkv_ref, ...), custom_call_target="tpu_custom_call" | custom-call | flops 4831838208 | bytes 11796480 | tf_op jit(solution)/shard_map/pallas_call | solution.py:186
  250.8 6.7 %fusion.65 = f32[1176,768]{1,0:T(8,128)} fusion(bf16[1176,1152]{1,0:T(8,128)(2,1)} %get-tuple-element.31, bf16[768,1152]{0,1:T(8,128)(2,1)} %bitcast.98), kind=kOutput, calls=%fused_computation.246 | convolution fusion | flops 2080899072 | bytes 8091648 | tf_op jit(solution)/shard_map/dot_general | solution.py:21
  269.7 22.5 %shard_map.274 = (bf16[1176,1152]{1,0:T(8,128)(2,1)}, f32[3,64,256]{2,1,0:T(8,128)}, f32[8,1152]{1,0:T(8,128)}) custom-call(bf16[1176,384]{1,0:T(8,128)(2,1)} %convolution_convert_fusion.6.grad_ref, bf16[1176,384]{1,0:T(8,128)(2,1)} %get-tuple-element.28.att_ref, bf16[24,64,1152]{2,1,0:T(8,128)(2,1)} %get-tuple-element.32.qkv_ref, ...), custom_call_target="tpu_custom_call" | custom-call | flops 4831838208 | bytes 11796480 | tf_op jit(solution)/shard_map/pallas_call | solution.py:186
  292.2 6.5 %convolution_convert_fusion.4 = bf16[768,1152]{1,0:T(8,128)(2,1)} fusion(bf16[1176,768]{1,0:T(8,128)(2,1)} %fusion.19.x_ref, bf16[1176,1152]{1,0:T(8,128)(2,1)} %get-tuple-element.34), kind=kOutput, calls=%fused_computation.56 | convolution fusion | flops 2081783808 | bytes 6285312 | tf_op jit(solution)/shard_map/dot_general | solution.py:25
  298.8 6.8 %fusion.24 = (f32[768]{0:T(1024)S(1)}, f32[1176]{0:T(1024)S(1)}, f32[1176]{0:T(1024)S(1)}, f32[768]{0:T(1024)S(1)}, f32[1176,768]{1,0:T(8,128)}) fusion(bf16[1176,768]{1,0:T(8,128)(2,1)S(1)} %copy-done.5, f32[1176]{0:T(1024)S(1)} %add_rsqrt_fusion.1, f32[1176]{0:T(1024)S(1)} %broadcast_multiply_fusion.5, f32[768]{0:T(1024)S(1)} %copy-done.47, ...), kind=kOutput, calls=%fused_computation.41 | convolution fusion | flops 2090830080 | bytes 13538688 | tf_op jit(solution)/shard_map/dot_general | solution.py:21
  317.9 7.8 %convolution_convert_fusion = bf16[1536,768]{1,0:T(8,128)(2,1)} fusion(bf16[1176,1536]{1,0:T(8,128)(2,1)} %get-tuple-element.108, bf16[1176,768]{1,0:T(8,128)(2,1)} %param.17, f32[1176]{0:T(1024)} %reshape.331), kind=kOutput, calls=%fused_computation.52 | convolution fusion | flops 2778421248 | bytes 7783008 | tf_op jit(solution)/shard_map/dot_general | solution.py:25
  380.5 7.2 %collective-permute-done.24 = bf16[384,1152]{1,0:T(8,128)(2,1)} collective-permute-done((bf16[384,1152]{1,0:T(8,128)(2,1)S(1)}, bf16[384,1152]{1,0:T(8,128)(2,1)}, u32[]{:S(2)}, u32[]{:S(2)}) %collective-permute-start.24) | collective-permute-done | bytes 884768 | tf_op jit(solution)/shard_map/ppermute | solution.py:308
  391.9 10.6 %collective-permute-done.25 = bf16[192,1152]{1,0:T(8,128)(2,1)S(1)} collective-permute-done((bf16[192,1152]{1,0:T(8,128)(2,1)S(1)}, bf16[192,1152]{1,0:T(8,128)(2,1)S(1)}, u32[]{:S(2)}, u32[]{:S(2)}) %collective-permute-start.25) | collective-permute-done | bytes 442400 | tf_op jit(solution)/shard_map/ppermute | solution.py:305
  412.6 18.7 %collective-permute-done.46 = bf16[384,1536]{1,0:T(8,128)(2,1)S(1)} collective-permute-done((bf16[384,1536]{1,0:T(8,128)(2,1)S(1)}, bf16[384,1536]{1,0:T(8,128)(2,1)S(1)}, u32[]{:S(2)}, u32[]{:S(2)}) %collective-permute-start.46) | collective-permute-done | bytes 1179680 | tf_op jit(solution)/shard_map/ppermute | solution.py:308
  440.2 15.1 %collective-permute-done.57 = bf16[768,768]{1,0:T(8,128)(2,1)S(1)} collective-permute-done((bf16[768,768]{1,0:T(8,128)(2,1)S(1)}, bf16[768,768]{1,0:T(8,128)(2,1)S(1)}, u32[]{:S(2)}, u32[]{:S(2)}) %collective-permute-start.57) | collective-permute-done | bytes 1179680 | tf_op jit(solution)/shard_map/ppermute | solution.py:308
  459.7 12.3 %collective-permute-done.58 = bf16[384,768]{1,0:T(8,128)(2,1)S(1)} collective-permute-done((bf16[384,768]{1,0:T(8,128)(2,1)S(1)}, bf16[384,768]{1,0:T(8,128)(2,1)S(1)}, u32[]{:S(2)}, u32[]{:S(2)}) %collective-permute-start.58) | collective-permute-done | bytes 589856 | tf_op jit(solution)/shard_map/ppermute | solution.py:305
  484.2 10.0 %collective-permute-done.60 = bf16[96,768]{1,0:T(8,128)(2,1)S(1)} collective-permute-done((bf16[96,768]{1,0:T(8,128)(2,1)S(1)}, bf16[96,768]{1,0:T(8,128)(2,1)S(1)}, u32[]{:S(2)}, u32[]{:S(2)}) %collective-permute-start.60) | collective-permute-done | bytes 147488 | tf_op jit(solution)/shard_map/ppermute | solution.py:305
  517.5 6.8 %dynamic_update_slice.112 = f32[768,1152]{0,1:T(8,128)} dynamic-update-slice(f32[768,1152]{0,1:T(8,128)} %broadcast_in_dim.36, f32[192,1152]{0,1:T(8,128)S(1)} %copy.45, s32[]{:T(128)S(6)} %select_n.611, s32[]{:T(128)} %constant.401.clone.1) | dynamic-update-slice | bytes 1769476 | tf_op jit(solution)/shard_map/dynamic_update_slice | solution.py:352
  525.6 7.7 %dynamic_update_slice.113 = f32[768,1152]{0,1:T(8,128)} dynamic-update-slice(f32[768,1152]{0,1:T(8,128)} %dynamic_update_slice.112, f32[192,1152]{0,1:T(8,128)S(1)} %copy.46, s32[]{:T(128)S(6)} %select_n.612, s32[]{:T(128)} %constant.401.clone.1) | dynamic-update-slice | bytes 1769476 | tf_op jit(solution)/shard_map/dynamic_update_slice | solution.py:352
  534.6 6.7 %dynamic_update_slice.114 = f32[768,1152]{0,1:T(8,128)} dynamic-update-slice(f32[768,1152]{0,1:T(8,128)} %dynamic_update_slice.113, f32[192,1152]{0,1:T(8,128)S(1)} %copy.47, s32[]{:T(128)S(6)} %select_n.613, s32[]{:T(128)} %constant.401.clone.1) | dynamic-update-slice | bytes 1769476 | tf_op jit(solution)/shard_map/dynamic_update_slice | solution.py:352
  542.5 7.0 %dynamic_update_slice.115 = f32[768,1152]{0,1:T(8,128)} dynamic-update-slice(f32[768,1152]{0,1:T(8,128)} %dynamic_update_slice.114, f32[192,1152]{0,1:T(8,128)S(1)} %copy.48, s32[]{:T(128)S(6)} %select_n.614, s32[]{:T(128)} %constant.401.clone.1) | dynamic-update-slice | bytes 1769476 | tf_op jit(solution)/shard_map/dynamic_update_slice | solution.py:352
  (473 shorter events, 272.7 us)
Async XLA Ops:
  3.2 32.7 %collective-permute-start.4 = (f32[40,128]{1,0:T(8,128)S(1)}, f32[40,128]{1,0:T(8,128)S(1)}, u32[]{:S(2)}, u32[]{:S(2)}) collective-permute-start(f32[40,128]{1,0:T(8,128)S(1)} %pad_bitcast_fusion.3), channel_id=1, source_target_pairs={{0,1},{1,0},{2,3},{3,2},{4,5},{5,4},{6,7},{7,6},{8,9},{9,8},{10,11... | collective-permute-start | bytes 61448 | tf_op jit(solution)/shard_map/ppermute | solution.py:308
  15.8 66.2 %collective-permute-start = (bf16[192,1152]{1,0:T(8,128)(2,1)}, bf16[192,1152]{1,0:T(8,128)(2,1)}, u32[]{:S(2)}, u32[]{:S(2)}) collective-permute-start(bf16[192,1152]{1,0:T(8,128)(2,1)} %constant_dynamic-slice_fusion.23), channel_id=1, source_target_pairs={{0,1},{1,0},{2,3},{3,2},{4,5},{5,4},{6,7},{7,6},{8,9},{9,8},{10,11... | collective-permute-start | bytes 1327112 | tf_op jit(solution)/shard_map/ppermute | solution.py:308
  17.4 58.0 %collective-permute-start.5 = (bf16[96,768]{1,0:T(8,128)(2,1)}, bf16[96,768]{1,0:T(8,128)(2,1)}, u32[]{:S(2)}, u32[]{:S(2)}) collective-permute-start(bf16[96,768]{1,0:T(8,128)(2,1)} %constant_dynamic-slice_fusion.22), channel_id=1, source_target_pairs={{0,1},{1,0},{2,3},{3,2},{4,5},{5,4},{6,7},{7,6},{8,9},{9,8},{10,11... | collective-permute-start | bytes 442376 | tf_op jit(solution)/shard_map/ppermute | solution.py:308
  20.2 66.7 %collective-permute-start.9 = (bf16[192,1536]{1,0:T(8,128)(2,1)}, bf16[192,1536]{1,0:T(8,128)(2,1)}, u32[]{:S(2)}, u32[]{:S(2)}) collective-permute-start(bf16[192,1536]{1,0:T(8,128)(2,1)} %constant_dynamic-slice_fusion.21), channel_id=1, source_target_pairs={{0,1},{1,0},{2,3},{3,2},{4,5},{5,4},{6,7},{7,6},{8,9},{9,8},{10,11... | collective-permute-start | bytes 1769480 | tf_op jit(solution)/shard_map/ppermute | solution.py:308
  22.2 68.9 %collective-permute-start.13 = (bf16[384,768]{1,0:T(8,128)(2,1)}, bf16[384,768]{1,0:T(8,128)(2,1)}, u32[]{:S(2)}, u32[]{:S(2)}) collective-permute-start(bf16[384,768]{1,0:T(8,128)(2,1)} %constant_dynamic-slice_fusion.20), channel_id=1, source_target_pairs={{0,1},{1,0},{2,3},{3,2},{4,5},{5,4},{6,7},{7,6},{8,9},{9,8},{10,11... | collective-permute-start | bytes 1769480 | tf_op jit(solution)/shard_map/ppermute | solution.py:308
  87.5 37.4 %collective-permute-start.11 = (bf16[192,1536]{1,0:T(8,128)(2,1)}, bf16[192,1536]{1,0:T(8,128)(2,1)S(1)}, u32[]{:S(2)}, u32[]{:S(2)}) collective-permute-start(bf16[192,1536]{1,0:T(8,128)(2,1)} %collective-permute-done.9), channel_id=1, source_target_pairs={{0,2},{2,0},{4,6},{6,4},{8,10},{10,8},{12,14},{14,12},{16,18},{18,... | collective-permute-start | bytes 1769480 | tf_op jit(solution)/shard_map/ppermute | solution.py:305
  91.1 29.0 %collective-permute-start.14 = (bf16[384,768]{1,0:T(8,128)(2,1)}, bf16[384,768]{1,0:T(8,128)(2,1)}, u32[]{:S(2)}, u32[]{:S(2)}) collective-permute-start(bf16[384,768]{1,0:T(8,128)(2,1)} %collective-permute-done.13), channel_id=1, source_target_pairs={{0,4},{2,6},{4,0},{6,2},{8,12},{10,14},{12,8},{14,10},{16,20},{18,... | collective-permute-start | bytes 1769480 | tf_op jit(solution)/shard_map/ppermute | solution.py:305
  96.1 26.0 %collective-permute-start.15 = (bf16[384,768]{1,0:T(8,128)(2,1)}, bf16[384,768]{1,0:T(8,128)(2,1)S(1)}, u32[]{:S(2)}, u32[]{:S(2)}) collective-permute-start(bf16[384,768]{1,0:T(8,128)(2,1)} %collective-permute-done.13), channel_id=1, source_target_pairs={{0,2},{2,0},{4,6},{6,4},{8,10},{10,8},{12,14},{14,12},{16,18},{18,... | collective-permute-start | bytes 1769480 | tf_op jit(solution)/shard_map/ppermute | solution.py:305
  97.1 28.7 %collective-permute-start.3 = (bf16[192,1152]{1,0:T(8,128)(2,1)S(1)}, bf16[192,1152]{1,0:T(8,128)(2,1)S(1)}, u32[]{:S(2)}, u32[]{:S(2)}) collective-permute-start(bf16[192,1152]{1,0:T(8,128)(2,1)S(1)} %collective-permute-done.1), channel_id=1, source_target_pairs={{0,2},{2,0},{4,6},{6,4},{8,10},{10,8},{12,14},{14,12},{16,18},{18,... | collective-permute-start | bytes 1327112 | tf_op jit(solution)/shard_map/ppermute | solution.py:305
  108.1 87.8 %collective-permute-start.12 = (bf16[192,1536]{1,0:T(8,128)(2,1)}, bf16[192,1536]{1,0:T(8,128)(2,1)}, u32[]{:S(2)}, u32[]{:S(2)}) collective-permute-start(bf16[192,1536]{1,0:T(8,128)(2,1)} %collective-permute-done.10), channel_id=1, source_target_pairs={{0,2},{2,0},{4,6},{6,4},{8,10},{10,8},{12,14},{14,12},{16,18},{18,... | collective-permute-start | bytes 1769480 | tf_op jit(solution)/shard_map/ppermute | solution.py:305
  120.2 84.0 %collective-permute-start.16 = (bf16[384,768]{1,0:T(8,128)(2,1)}, bf16[384,768]{1,0:T(8,128)(2,1)}, u32[]{:S(2)}, u32[]{:S(2)}) collective-permute-start(bf16[384,768]{1,0:T(8,128)(2,1)} %collective-permute-done.14), channel_id=1, source_target_pairs={{0,2},{2,0},{4,6},{6,4},{8,10},{10,8},{12,14},{14,12},{16,18},{18,... | collective-permute-start | bytes 1769480 | tf_op jit(solution)/shard_map/ppermute | solution.py:305
  191.2 220.3 %collective-permute-start.44 = (bf16[384,1536]{1,0:T(8,128)(2,1)}, bf16[384,1536]{1,0:T(8,128)(2,1)}, u32[]{:S(2)}, u32[]{:S(2)}) collective-permute-start(bf16[384,1536]{1,0:T(8,128)(2,1)} %constant_dynamic-slice_fusion.9), channel_id=1, source_target_pairs={{0,2},{2,0},{4,6},{6,4},{8,10},{10,8},{12,14},{14,12},{16,18},{18,... | collective-permute-start | bytes 3538952 | tf_op jit(solution)/shard_map/ppermute | solution.py:305
  311.8 26.0 %collective-permute-start.17 = (f32[80,128]{1,0:T(8,128)S(1)}, f32[80,128]{1,0:T(8,128)S(1)}, u32[]{:S(2)}, u32[]{:S(2)}) collective-permute-start(f32[80,128]{1,0:T(8,128)S(1)} %pad_maximum_fusion.8), channel_id=1, source_target_pairs={{0,1},{1,0},{2,3},{3,2},{4,5},{5,4},{6,7},{7,6},{8,9},{9,8},{10,11... | collective-permute-start | bytes 122888 | tf_op jit(solution)/shard_map/ppermute | solution.py:308
  338.1 29.8 %collective-permute-start.23 = (bf16[384,1152]{1,0:T(8,128)(2,1)S(1)}, bf16[384,1152]{1,0:T(8,128)(2,1)S(1)}, u32[]{:S(2)}, u32[]{:S(2)}) collective-permute-start(bf16[384,1152]{1,0:T(8,128)(2,1)S(1)} %constant_dynamic-slice_fusion.18), channel_id=1, source_target_pairs={{0,2},{2,0},{4,6},{6,4},{8,10},{10,8},{12,14},{14,12},{16,18},{18,... | collective-permute-start | bytes 2654216 | tf_op jit(solution)/shard_map/ppermute | solution.py:305
  348.9 31.2 %collective-permute-start.22 = (bf16[384,1152]{1,0:T(8,128)(2,1)}, bf16[384,1152]{1,0:T(8,128)(2,1)}, u32[]{:S(2)}, u32[]{:S(2)}) collective-permute-start(bf16[384,1152]{1,0:T(8,128)(2,1)} %constant_dynamic-slice_fusion.19), channel_id=1, source_target_pairs={{0,2},{2,0},{4,6},{6,4},{8,10},{10,8},{12,14},{14,12},{16,18},{18,... | collective-permute-start | bytes 2654216 | tf_op jit(solution)/shard_map/ppermute | solution.py:305
  360.2 29.6 %collective-permute-start.45 = (bf16[384,1536]{1,0:T(8,128)(2,1)}, bf16[384,1536]{1,0:T(8,128)(2,1)S(1)}, u32[]{:S(2)}, u32[]{:S(2)}) collective-permute-start(bf16[384,1536]{1,0:T(8,128)(2,1)} %constant_dynamic-slice_fusion.8), channel_id=1, source_target_pairs={{0,2},{2,0},{4,6},{6,4},{8,10},{10,8},{12,14},{14,12},{16,18},{18,... | collective-permute-start | bytes 3538952 | tf_op jit(solution)/shard_map/ppermute | solution.py:305
  379.9 60.3 %collective-permute-start.55 = (bf16[768,768]{1,0:T(8,128)(2,1)S(1)}, bf16[768,768]{1,0:T(8,128)(2,1)S(1)}, u32[]{:S(2)}, u32[]{:S(2)}) collective-permute-start(bf16[768,768]{1,0:T(8,128)(2,1)S(1)} %copy-done.29), channel_id=1, source_target_pairs={{0,2},{2,0},{4,6},{6,4},{8,10},{10,8},{12,14},{14,12},{16,18},{18,... | collective-permute-start | bytes 3538952 | tf_op jit(solution)/shard_map/ppermute | solution.py:305
  387.7 126.4 %collective-permute-start.43 = (bf16[96,768]{1,0:T(8,128)(2,1)}, bf16[96,768]{1,0:T(8,128)(2,1)S(1)}, u32[]{:S(2)}, u32[]{:S(2)}) collective-permute-start(bf16[96,768]{1,0:T(8,128)(2,1)} %collective-permute-done.41), channel_id=1, source_target_pairs={{0,2},{2,0},{4,6},{6,4},{8,10},{10,8},{12,14},{14,12},{16,18},{18,... | collective-permute-start | bytes 442376 | tf_op jit(solution)/shard_map/ppermute | solution.py:305
  402.5 28.8 %collective-permute-start.46 = (bf16[384,1536]{1,0:T(8,128)(2,1)S(1)}, bf16[384,1536]{1,0:T(8,128)(2,1)S(1)}, u32[]{:S(2)}, u32[]{:S(2)}) collective-permute-start(bf16[384,1536]{1,0:T(8,128)(2,1)S(1)} %add_convert_fusion.5), channel_id=1, source_target_pairs={{0,1},{1,0},{2,3},{3,2},{4,5},{5,4},{6,7},{7,6},{8,9},{9,8},{10,11... | collective-permute-start | bytes 3538952 | tf_op jit(solution)/shard_map/ppermute | solution.py:308
  410.9 44.3 %collective-permute-start.57 = (bf16[768,768]{1,0:T(8,128)(2,1)S(1)}, bf16[768,768]{1,0:T(8,128)(2,1)S(1)}, u32[]{:S(2)}, u32[]{:S(2)}) collective-permute-start(bf16[768,768]{1,0:T(8,128)(2,1)S(1)} %add_convert_fusion.2), channel_id=1, source_target_pairs={{0,1},{1,0},{2,3},{3,2},{4,5},{5,4},{6,7},{7,6},{8,9},{9,8},{10,11... | collective-permute-start | bytes 3538952 | tf_op jit(solution)/shard_map/ppermute | solution.py:308
  458.8 74.5 %collective-permute-start.31 = (bf16[192,1152]{1,0:T(8,128)(2,1)}, bf16[192,1152]{1,0:T(8,128)(2,1)}, u32[]{:S(2)}, u32[]{:S(2)}) collective-permute-start(bf16[192,1152]{1,0:T(8,128)(2,1)} %get-tuple-element.71), channel_id=1, source_target_pairs={{0,2},{2,0},{4,6},{6,4},{8,10},{10,8},{12,14},{14,12},{16,18},{18,... | collective-permute-start | bytes 1327112 | tf_op jit(solution)/shard_map/ppermute | solution.py:305
  481.3 60.0 %collective-permute-start.32 = (bf16[192,1152]{1,0:T(8,128)(2,1)}, bf16[192,1152]{1,0:T(8,128)(2,1)}, u32[]{:S(2)}, u32[]{:S(2)}) collective-permute-start(bf16[192,1152]{1,0:T(8,128)(2,1)} %collective-permute-done.30), channel_id=1, source_target_pairs={{0,2},{2,0},{4,6},{6,4},{8,10},{10,8},{12,14},{14,12},{16,18},{18,... | collective-permute-start | bytes 1327112 | tf_op jit(solution)/shard_map/ppermute | solution.py:305
  508.8 47.5 %collective-permute-start.52 = (bf16[192,1536]{1,0:T(8,128)(2,1)}, bf16[192,1536]{1,0:T(8,128)(2,1)}, u32[]{:S(2)}, u32[]{:S(2)}) collective-permute-start(bf16[192,1536]{1,0:T(8,128)(2,1)} %pad_maximum_fusion), channel_id=1, source_target_pairs={{0,4},{2,6},{4,0},{6,2},{8,12},{10,14},{12,8},{14,10},{16,20},{18,... | collective-permute-start | bytes 1769480 | tf_op jit(solution)/shard_map/ppermute | solution.py:305
  512.5 43.8 %collective-permute-start.63 = (bf16[384,768]{1,0:T(8,128)(2,1)}, bf16[384,768]{1,0:T(8,128)(2,1)}, u32[]{:S(2)}, u32[]{:S(2)}) collective-permute-start(bf16[384,768]{1,0:T(8,128)(2,1)} %pad_maximum_fusion.1), channel_id=1, source_target_pairs={{0,4},{2,6},{4,0},{6,2},{8,12},{10,14},{12,8},{14,10},{16,20},{18,... | collective-permute-start | bytes 1769480 | tf_op jit(solution)/shard_map/ppermute | solution.py:305
  (108 other events, 983.9 us)
